TPU v7x, 128 devices: a whole 4x4x4 slice. The times are simulated.
128 devices in a mesh: mp: 8 (over x, z_lo), item: 16 (over z_hi, y, core).
Axes of the slice: x: 4, y: 4, z: 4 (z_hi: 2, z_lo: 2; z = z_hi * 2 + z_lo), core: 2. Of those that a mesh axis runs over, the one named last changes fastest.
Arguments:
- response: int32 [16384, 32768], P('mp', 'item'), may hold values from 0 to 2
- difficulty: float32 [32768], P('item'), may hold values from -4 to 4
- ability: float32 [16384, 256], P('mp', 'item'), may hold values from -6 to 6
- ability_m: float32 [16384, 256], P('mp', 'item'), may hold values from -3 to 3
- ability_v: float32 [16384, 256], P('mp', 'item'), may hold values from 0.02 to 0.5
- discrim: float32 [32768, 256], P('item', 'mp'), may hold values from -0.375 to 0.375
- discrim_m: float32 [32768, 256], P('item', 'mp'), may hold values from -3 to 3
- discrim_v: float32 [32768, 256], P('item', 'mp'), may hold values from 0.02 to 0.5
Outputs:
- ability_new: float32 [16384, 256], P('mp', 'item')
- ability_m_new: float32 [16384, 256], P('mp', 'item')
- ability_v_new: float32 [16384, 256], P('mp', 'item')
- discrim_new: float32 [32768, 256], P('item', 'mp')
- discrim_m_new: float32 [32768, 256], P('item', 'mp')
- discrim_v_new: float32 [32768, 256], P('item', 'mp')
Inputs may be any that keep to these rules, and one draw needn't show every extreme that they name: `response`: 0 marks an unobserved pair, 1 an observed wrong answer, 2 an observed right answer.
All inputs are finite; a program needn't handle non-finite values.
Results may differ from a plain program's by a relative error of at most 0.0012.
Values may be sent and summed in bfloat16 or wider, within the bound.
A program may use at most 128 MiB of HBM per device.

v0:
```python
import math

import jax
import jax.numpy as jnp
from jax import lax
from jax.sharding import PartitionSpec as P

K = 256


beta_one = 0.9
beta_two = 0.999
corr_one = 1.0 - 0.9**10
corr_two = 1.0 - 0.999**10
adam_eps = 1e-08


def adam_update(factor, moment, second, gradient, step_rate):
    moment_new = beta_one * moment + (1.0 - beta_one) * gradient
    second_new = beta_two * second + (1.0 - beta_two) * gradient * gradient
    update = moment_new / corr_one / (jnp.sqrt(second_new / corr_two) + adam_eps)
    return (factor - step_rate * update, moment_new, second_new)


def shards(response, difficulty, ability, ability_m, ability_v, discrim, discrim_m, discrim_v):
    ability_full = lax.all_gather(ability.astype(jnp.bfloat16), "item", axis=1, tiled=True)
    discrim_full = lax.all_gather(discrim.astype(jnp.bfloat16), "mp", axis=1, tiled=True)
    logits = lax.dot_general(
        ability_full, discrim_full, (((1,), (1,)), ((), ())), preferred_element_type=jnp.float32
    )
    logits = logits + difficulty[None, :]
    correct = (response == 2).astype(jnp.float32)
    residual = jnp.where(response > 0, jax.nn.sigmoid(logits) - correct, jnp.float32(0.0))
    ability_wide = ability_full.astype(jnp.float32)
    discrim_wide = discrim_full.astype(jnp.float32)
    highest = lax.Precision.HIGHEST
    ability_cols = ability.shape[1]
    discrim_cols = discrim.shape[1]
    items_total = response.shape[1] * lax.axis_size("item")
    ckpts_total = response.shape[0] * lax.axis_size("mp")
    ability_partial = jnp.dot(residual, discrim_wide, precision=highest)
    ability_sum = lax.psum(ability_partial, "item")
    ability_grad = lax.dynamic_slice_in_dim(
        ability_sum, lax.axis_index("item") * ability_cols, ability_cols, 1
    )
    discrim_partial = lax.dot_general(
        residual, ability_wide, (((0,), (0,)), ((), ())), precision=highest
    )
    discrim_sum = lax.psum(discrim_partial, "mp")
    discrim_grad = lax.dynamic_slice_in_dim(
        discrim_sum, lax.axis_index("mp") * discrim_cols, discrim_cols, 1
    )
    ability_grad = ability_grad * math.sqrt(K / items_total)
    discrim_grad = discrim_grad * math.sqrt(1.0 / ckpts_total)
    ability_new, ability_m_new, ability_v_new = adam_update(
        ability, ability_m, ability_v, ability_grad, 0.05
    )
    discrim_new, discrim_m_new, discrim_v_new = adam_update(
        discrim, discrim_m, discrim_v, discrim_grad, 0.01
    )
    return (ability_new, ability_m_new, ability_v_new, discrim_new, discrim_m_new, discrim_v_new)


def solution(mesh):
    return jax.shard_map(
        shards,
        mesh=mesh,
        in_specs=(
            P("mp", "item"),
            P("item"),
            P("mp", "item"),
            P("mp", "item"),
            P("mp", "item"),
            P("item", "mp"),
            P("item", "mp"),
            P("item", "mp"),
        ),
        out_specs=(
            P("mp", "item"),
            P("mp", "item"),
            P("mp", "item"),
            P("item", "mp"),
            P("item", "mp"),
            P("item", "mp"),
        ),
        check_vma=False,
    )
```

profile of v0, /device:TPU:0, one launch (start us, length us, event | category | flops | bytes accessed | tf_op | source)
XLA Modules:
  0.0 386.4 jit_solution(2040958627910483739)
XLA Ops:
  7.2 0.0 all-gather.5.cloned.1.call-start
  7.2 1.6 convert_element_type.12
  8.8 0.0 all-gather.5.cloned.1.call-update
  8.9 0.0 all-gather.3.cloned.1.call-start
  8.9 1.5 convert_element_type.11
  10.5 0.0 all-gather.3.cloned.1.call-update
  10.5 0.0 all-reduce.3.cloned.1.call-start
  10.5 41.0 %all-gather.5.cloned.1.call-done = bf16[2048,256]{0,1:T(8,128)(2,1)} async-done(((bf16[2048,32]{0,1:T(8,128)(2,1)}), bf16[2048,256]{0,1:T(8,128)(2,1)}) %all-gather.5.cloned.1.call-update) | async-done | bytes 1048592 | tf_op jit(solution)/shard_map/all_gather | solution.py:27
  51.5 0.0 copy-start.2
  51.6 47.8 %all-gather.3.cloned.1.call-done = bf16[2048,256]{0,1:T(8,128)(2,1)} async-done(((bf16[2048,16]{0,1:T(8,128)(2,1)}), bf16[2048,256]{0,1:T(8,128)(2,1)}) %all-gather.3.cloned.1.call-update) | async-done | bytes 1048592 | tf_op jit(solution)/shard_map/all_gather | solution.py:26
  99.3 12.1 %subtract_select_fusion = f32[2048,2048]{1,0:T(8,128)S(1)} fusion(s32[2048,2048]{1,0:T(8,128)} %param.8, bf16[2048,256]{0,1:T(8,128)(2,1)} %all-gather.3.cloned.1.call-done, bf16[2048,256]{0,1:T(8,128)(2,1)} %all-gather.5.cloned.1.call-done, f32[2048]{0:T(1024)} %param.9), kind=kOutput, calls=%fused_computation | convolution fusion | flops 2185232384 | bytes 35659776 | tf_op jit(solution)/shard_map/dot_general | solution.py:28
  111.5 0.0 copy-start
  111.5 5.7 %copy-done = f32[2048,2048]{1,0:T(8,128)} copy-done((f32[2048,2048]{1,0:T(8,128)}, f32[2048,2048]{1,0:T(8,128)S(1)}, u32[]{:S(2)}) %copy-start) | copy-done | bytes 16777240
  117.2 0.0 copy-done.2
  117.2 0.0 copy-start.1
  117.2 9.8 %fusion = f32[2048,256]{0,1:T(8,128)} fusion(f32[2048,2048]{1,0:T(8,128)S(1)} %subtract_select_fusion, bf16[2048,256]{0,1:T(8,128)(2,1)S(1)} %copy-done.2), kind=kOutput, calls=%fused_computation.7 | convolution fusion | flops 12884901888 | bytes 19922944 | tf_op jit(solution)/shard_map/dot_general | solution.py:41
  127.0 0.0 copy-start.4
  127.0 0.0 copy-start.7
  127.0 0.0 copy-start.8
  127.0 0.0 copy-start.3
  127.0 0.0 copy-start.5
  127.0 0.0 copy-start.6
  127.0 0.0 all-reduce.3.cloned.1.call-update
  127.0 0.2 all-reduce.5.cloned.1.call-start
  127.3 0.0 copy-done.1
  127.3 13.3 %fusion.1 = f32[2048,256]{0,1:T(8,128)} fusion(f32[2048,2048]{1,0:T(8,128)} %copy-done, bf16[2048,256]{0,1:T(8,128)(2,1)S(1)} %copy-done.1), kind=kOutput, calls=%fused_computation.8 | convolution fusion | flops 12884901888 | bytes 19922944 | tf_op jit(solution)/shard_map/dot_general | solution.py:46
  140.6 0.0 all-reduce.5.cloned.1.call-update
  140.6 129.7 %all-reduce.3.cloned.1.call-done = f32[2048,256]{0,1:T(8,128)} async-done(((f32[2048,256]{0,1:T(8,128)}), f32[2048,256]{0,1:T(8,128)}) %all-reduce.3.cloned.1.call-update) | async-done | bytes 2097168 | tf_op jit(solution)/shard_map/psum | solution.py:42
  270.3 0.0 copy-done.4
  270.3 0.0 copy-done.7
  270.3 0.0 copy-done.8
  270.3 1.7 multiply_subtract_fusion.1
  272.0 105.9 %all-reduce.5.cloned.1.call-done = f32[2048,256]{0,1:T(8,128)} async-done(((f32[2048,256]{0,1:T(8,128)}), f32[2048,256]{0,1:T(8,128)}) %all-reduce.5.cloned.1.call-update) | async-done | bytes 2097168 | tf_op jit(solution)/shard_map/psum | solution.py:49
  377.9 0.0 copy-done.3
  377.9 0.0 copy-done.5
  377.9 0.0 copy-done.6
  377.9 1.9 multiply_subtract_fusion
Async XLA Ops:
  7.2 44.4 %all-gather.5.cloned.1.call-start = ((), (), s32[]{:S(2)}) async-start(), calls=%async_computation.1 | async-start | bytes 1179648 | tf_op jit(solution)/shard_map/all_gather | solution.py:27
  8.9 90.5 %all-gather.3.cloned.1.call-start = ((), (), s32[]{:S(2)}) async-start(), calls=%async_computation | async-start | bytes 1114112 | tf_op jit(solution)/shard_map/all_gather | solution.py:26
  10.5 259.8 %all-reduce.3.cloned.1.call-start = ((), (), s32[]{:S(2)}) async-start(), calls=%async_computation.2 | async-start | bytes 4194304 | tf_op jit(solution)/shard_map/psum | solution.py:42
  51.5 65.7 %copy-start.2 = (bf16[2048,256]{0,1:T(8,128)(2,1)S(1)}, bf16[2048,256]{0,1:T(8,128)(2,1)}, u32[]{:S(2)}) copy-start(bf16[2048,256]{0,1:T(8,128)(2,1)} %all-gather.5.cloned.1.call-done) | copy-start | bytes 3145732
  111.5 5.7 %copy-start = (f32[2048,2048]{1,0:T(8,128)}, f32[2048,2048]{1,0:T(8,128)S(1)}, u32[]{:S(2)}) copy-start(f32[2048,2048]{1,0:T(8,128)S(1)} %subtract_select_fusion) | copy-start | bytes 50331652
  117.2 10.1 %copy-start.1 = (bf16[2048,256]{0,1:T(8,128)(2,1)S(1)}, bf16[2048,256]{0,1:T(8,128)(2,1)}, u32[]{:S(2)}) copy-start(bf16[2048,256]{0,1:T(8,128)(2,1)} %all-gather.3.cloned.1.call-done) | copy-start | bytes 3145732
  127.0 143.3 %copy-start.4 = (f32[2048,16]{0,1:T(8,128)S(1)}, f32[2048,16]{0,1:T(8,128)}, u32[]{:S(2)}) copy-start(f32[2048,16]{0,1:T(8,128)} %param.10) | copy-start | bytes 393220
  127.0 143.3 %copy-start.7 = (f32[2048,16]{0,1:T(8,128)S(1)}, f32[2048,16]{0,1:T(8,128)}, u32[]{:S(2)}) copy-start(f32[2048,16]{0,1:T(8,128)} %param.11) | copy-start | bytes 393220
  127.0 143.3 %copy-start.8 = (f32[2048,16]{0,1:T(8,128)S(1)}, f32[2048,16]{0,1:T(8,128)}, u32[]{:S(2)}) copy-start(f32[2048,16]{0,1:T(8,128)} %param.12) | copy-start | bytes 393220
  127.0 250.9 %copy-start.3 = (f32[2048,32]{0,1:T(8,128)S(1)}, f32[2048,32]{0,1:T(8,128)}, u32[]{:S(2)}) copy-start(f32[2048,32]{0,1:T(8,128)} %param.13) | copy-start | bytes 786436
  127.0 250.9 %copy-start.5 = (f32[2048,32]{0,1:T(8,128)S(1)}, f32[2048,32]{0,1:T(8,128)}, u32[]{:S(2)}) copy-start(f32[2048,32]{0,1:T(8,128)} %param.14) | copy-start | bytes 786436
  127.0 250.9 %copy-start.6 = (f32[2048,32]{0,1:T(8,128)S(1)}, f32[2048,32]{0,1:T(8,128)}, u32[]{:S(2)}) copy-start(f32[2048,32]{0,1:T(8,128)} %param.15) | copy-start | bytes 786436
  127.0 250.9 %all-reduce.5.cloned.1.call-start = ((), (), s32[]{:S(2)}) async-start(), calls=%async_computation.3 | async-start | bytes 4194304 | tf_op jit(solution)/shard_map/psum | solution.py:49
Sparse Core Ops, SparseCore 0:
  10.2 41.3 all-gather.4
  54.6 44.7 all-gather.2
  127.2 143.0 all-reduce.2
  272.7 105.1 all-reduce.4
where the time goes:
time: 387 us; the launch traced here: 386 us
  waiting for transfers between devices  324 us (84%)
  matrix products  35.2 us (9%)
  between operations  13.8 us (4%)
  other arithmetic  6.8 us (2%)
  local copies, waits for them, and re-layouts  5.78 us (1%)
    psum x1, waiting for transfers between devices, shards(): ability_sum = lax.psum(ability_partial, 'item')  130 us
    psum x1, waiting for transfers between devices, shards(): discrim_sum = lax.psum(discrim_partial, 'mp')  106 us
    all_gather x1, waiting for transfers between devices, shards(): lax.all_gather(ability.astype(jnp.bfloat16), 'item', axis=1, tiled=True)  47.8 us
    all_gather x1, waiting for transfers between devices, shards(): lax.all_gather(discrim.astype(jnp.bfloat16), 'mp', axis=1, tiled=True)  41 us
    dot_general x1, matrix products, shards(): lax.dot_general(residual, ability_wide, (((0,), (0,)), ((), ())), precisi...  13.3 us
    dot_general x1, matrix products, shards(): lax.dot_general(ability_full, discrim_full, (((1,), (1,)), ((), ())), pre...  12.1 us
    dot_general x1, matrix products, shards(): ability_partial = jnp.dot(residual, discrim_wide, precision=highest)  9.76 us
  transfers between devices with their start and end apart: 4, of which 4 were waited for; matrix products, arithmetic and copies ran while one was open for 4% of the time, Pallas kernels for 0%

commit v1 on v0

v1 whole, which is shorter than its diff:
```python
import math

import jax
import jax.numpy as jnp
from jax import lax
from jax.experimental import pallas as pl
from jax.experimental.pallas import tpu as pltpu
from jax.sharding import PartitionSpec as P

K = 256
N = 2048
RH, CJ = 1024, 512
NR, NJ = N // RH, N // CJ
RING = 4
DB, AB = 32, 16

TILES = ((0, 0), (1, 0), (0, 1), (1, 1), (2, 0), (3, 0), (2, 1), (3, 1))

D_MSG, A_MSG, C_MSG, RD_MSG, RA_MSG = 8, 9, 8, 8, 9
BASE_D = 0
BASE_A = BASE_D + NJ * D_MSG
BASE_C = BASE_A + NR * A_MSG
BASE_RD = BASE_C + NR * C_MSG
BASE_RA = BASE_RD + NJ * RD_MSG
BASE_RC = BASE_RA + NR * RA_MSG
N_SEM = BASE_RC + NR

beta_one = 0.9
beta_two = 0.999
corr_one = 1.0 - 0.9**10
corr_two = 1.0 - 0.999**10
adam_eps = 1e-08

BF = jnp.bfloat16
F32 = jnp.float32


def adam_update(factor, moment, second, gradient, step_rate):
    moment_new = beta_one * moment + (1.0 - beta_one) * gradient
    second_new = beta_two * second + (1.0 - beta_two) * gradient * gradient
    update = moment_new / corr_one / (jnp.sqrt(second_new / corr_two) + adam_eps)
    return (factor - step_rate * update, moment_new, second_new)


def kernel(
    ability_ref, discrim_ref, diff_ref, resp_ref, ga_out, gd_out,
    at, asc, dt, rv, ga, gd, rb, sd, rd, sa, ra, cs, cr,
    send_sem, recv_sem, resp_sem,
):
    mp, item = lax.axis_index("mp"), lax.axis_index("item")
    x, p = mp // 2, mp % 2
    z, y, c = item // 8, (item // 2) % RING, item % 2

    def mp_dev(dx, flip):
        return {"mp": ((x + dx) % RING) * 2 + (1 - p if flip else p)}

    def item_dev(dy, flip):
        return {"item": ((1 - z if flip else z) * RING + (y + dy) % RING) * 2 + c}

    x_next, x_prev, x_pair = mp_dev(1, False), mp_dev(RING - 1, False), mp_dev(0, True)
    y_next, y_prev, y_pair = item_dev(1, False), item_dev(RING - 1, False), item_dev(0, True)
    core = {"item": item + 1 - 2 * c}

    sent = []

    def message(index, src, dst, device):
        return pltpu.make_async_remote_copy(
            src_ref=src, dst_ref=dst, send_sem=send_sem.at[index], recv_sem=recv_sem.at[index],
            device_id=device, device_id_type=pl.DeviceIdType.MESH,
        )

    landed = {}

    def send(index, src, dst, device):
        copy = message(index, src, dst, device)
        copy.start()
        sent.append(copy)
        landed[index] = copy

    def arrive(index):
        landed[index].wait_recv()

    def d_rows(dx, flip):
        block = ((x + dx) % RING) * 2 + (1 - p if flip else p)
        return pl.multiple_of(block * DB, DB)

    def d_block(j, dx, flip):
        return dt.at[j, pl.ds(d_rows(dx, flip), DB), :]

    def d_half(j, dx, flip, half):
        return dt.at[j, pl.ds(pl.multiple_of(d_rows(dx, flip) + half * (DB // 2), DB // 2), DB // 2), :]

    def d_send(j, m, ref, device):
        send(BASE_D + j * D_MSG + m, ref, ref, device)

    def d_wait(j, m):
        arrive(BASE_D + j * D_MSG + m)

    def d_step0(j):
        own = d_block(j, 0, False)
        d_send(j, 0, own, x_pair)
        d_send(j, 1, own, x_next)
        d_send(j, 2, own, x_prev)

    def d_step1(j):
        d_wait(j, 0)
        other = d_block(j, 0, True)
        d_send(j, 3, other, x_next)
        d_send(j, 4, other, x_prev)
        d_wait(j, 1)
        d_send(j, 5, d_half(j, RING - 1, False, 0), x_next)
        d_wait(j, 2)
        d_send(j, 6, d_half(j, 1, False, 1), x_prev)

    def d_step2(j):
        d_wait(j, 5)
        d_wait(j, 6)
        d_send(j, 7, d_block(j, 2, False), x_pair)

    def d_done(j):
        d_wait(j, 3)
        d_wait(j, 4)
        d_wait(j, 7)

    def a_rows(dy, flip, which):
        chip = (1 - z if flip else z) * RING + (y + dy) % RING
        return pl.multiple_of((chip * 2 + which) * AB, AB)

    def a_block(r, dy, flip):
        return at.at[r, pl.ds(a_rows(dy, flip, c), AB), :]

    def a_half(r, dy, flip, half):
        return at.at[r, pl.ds(a_rows(dy, flip, c), AB), half * (RH // 2) : (half + 1) * (RH // 2)]

    def a_send(r, m, ref, device):
        send(BASE_A + r * A_MSG + m, ref, ref, device)

    def a_wait(r, m):
        arrive(BASE_A + r * A_MSG + m)

    def c_send(r, m, ref):
        send(BASE_C + r * C_MSG + m, ref, ref, core)

    def a_step0(r):
        own = a_block(r, 0, False)
        a_send(r, 0, own, y_pair)
        a_send(r, 1, own, y_next)
        a_send(r, 2, own, y_prev)
        c_send(r, 0, own)

    def a_step1(r):
        a_wait(r, 1)
        a_send(r, 5, a_half(r, RING - 1, False, 0), y_next)
        a_wait(r, 2)
        a_send(r, 6, a_half(r, 1, False, 1), y_prev)
        c_send(r, 2, a_block(r, RING - 1, False))
        c_send(r, 3, a_block(r, 1, False))
        a_wait(r, 0)
        other = a_block(r, 0, True)
        a_send(r, 3, other, y_next)
        a_send(r, 4, other, y_prev)
        c_send(r, 1, other)

    def a_step2(r):
        a_wait(r, 3)
        a_send(r, 7, a_half(r, RING - 1, True, 0), y_next)
        a_wait(r, 4)
        a_send(r, 8, a_half(r, 1, True, 1), y_prev)
        c_send(r, 4, a_block(r, RING - 1, True))
        c_send(r, 5, a_block(r, 1, True))

    def a_step3(r):
        a_wait(r, 5)
        a_wait(r, 6)
        c_send(r, 6, a_block(r, 2, False))
        a_wait(r, 7)
        a_wait(r, 8)
        c_send(r, 7, a_block(r, 2, True))

    def a_done(r):
        for m in range(C_MSG):
            arrive(BASE_C + r * C_MSG + m)
        for i in range(RH // 512):
            part = at[r, :, i * 512 : (i + 1) * 512].astype(F32) * 0.5
            asc[r, i * 512 : (i + 1) * 512, :] = part.T.astype(BF)

    def rd_send(j, m, value, device):
        sd[j, m] = value.astype(BF)
        send(BASE_RD + j * RD_MSG + m, sd.at[j, m], rd.at[j, m], device)

    def rd_send_half(j, m, value, device):
        sd[j, m, 0 : DB // 2] = value.astype(BF)
        send(
            BASE_RD + j * RD_MSG + m, sd.at[j, m, pl.ds(0, DB // 2)], rd.at[j, m, pl.ds(0, DB // 2)], device
        )

    def rd_wait(j, m):
        arrive(BASE_RD + j * RD_MSG + m)

    def d_part(j, dx, flip):
        return gd[j, pl.ds(d_rows(dx, flip), DB), :]

    def rd_step1(j):
        rd_send(j, 1, d_part(j, 1, True), x_next)
        rd_send(j, 2, d_part(j, RING - 1, True), x_prev)
        rd_send(j, 0, d_part(j, 2, True), x_pair)

    def rd_step2(j):
        rd_wait(j, 0)
        far = d_part(j, 2, False) + rd[j, 0].astype(F32)
        rd_send_half(j, 3, far[: DB // 2], x_next)
        rd_send_half(j, 4, far[DB // 2 :], x_prev)
        rd_wait(j, 1)
        rd_wait(j, 2)
        rd_send(j, 5, d_part(j, 0, True) + rd[j, 1].astype(F32) + rd[j, 2].astype(F32), x_pair)

    def rd_step3(j):
        rd_wait(j, 3)
        near = d_part(j, 1, False)
        rd_send(
            j, 6,
            jnp.concatenate([near[: DB // 2] + rd[j, 3, 0 : DB // 2].astype(F32), near[DB // 2 :]], axis=0),
            x_next,
        )
        rd_wait(j, 4)
        near = d_part(j, RING - 1, False)
        rd_send(
            j, 7,
            jnp.concatenate([near[: DB // 2], near[DB // 2 :] + rd[j, 4, 0 : DB // 2].astype(F32)], axis=0),
            x_prev,
        )

    d_scale = 0.5 * math.sqrt(1.0 / 16384)
    a_scale = 0.5 * math.sqrt(K / 32768)

    def rd_final(j):
        for m in (5, 6, 7):
            rd_wait(j, m)
        total = d_part(j, 0, False) + rd[j, 5].astype(F32) + rd[j, 6].astype(F32) + rd[j, 7].astype(F32)
        gd_out[:, j * CJ : (j + 1) * CJ] = total * d_scale

    H = RH // 2

    def ra_core(r):
        for b in range(8):
            rows = pl.ds(pl.multiple_of(b * 2 * AB + (1 - c) * AB, AB), AB)
            cs[r, b] = ga[r, rows, :].astype(BF)
        send(BASE_RC + r, cs.at[r], cr.at[r], core)

    def a_part(r, dy, flip, half):
        return ga[r, pl.ds(a_rows(dy, flip, c), AB), half * H : (half + 1) * H]

    def ra_start(r, m, halves, device):
        lo, n = halves
        ref = lambda buf: buf.at[r, m, pl.ds(lo, n)]
        send(BASE_RA + r * RA_MSG + m, ref(sa), ref(ra), device)

    def ra_half(r, m, half, value, device):
        sa[r, m, half] = value.astype(BF)
        ra_start(r, m, (half, 1), device)

    def ra_full(r, m, values, device):
        for half in range(2):
            sa[r, m, half] = values[half].astype(BF)
        ra_start(r, m, (0, 2), device)

    def ra_wait(r, m):
        arrive(BASE_RA + r * RA_MSG + m)

    def ra_step1(r):
        arrive(BASE_RC + r)
        for b in range(8):
            rows = pl.ds(pl.multiple_of(b * 2 * AB + c * AB, AB), AB)
            ga[r, rows, :] += cr[r, b].astype(F32)
        ra_half(r, 0, 0, a_part(r, 2, True, 0), y_next)
        ra_half(r, 1, 1, a_part(r, 2, True, 1), y_prev)
        ra_half(r, 2, 0, a_part(r, 2, False, 0), y_next)
        ra_half(r, 3, 1, a_part(r, 2, False, 1), y_prev)

    def ra_step2(r):
        for first, flip in ((0, True), (2, False)):
            ra_wait(r, first)
            ra_full(
                r, 4 + first,
                (a_part(r, 1, flip, 0) + ra[r, first, 0].astype(F32), a_part(r, 1, flip, 1)), y_next,
            )
            ra_wait(r, first + 1)
            ra_full(
                r, 5 + first,
                (a_part(r, RING - 1, flip, 0), a_part(r, RING - 1, flip, 1) + ra[r, first + 1, 1].astype(F32)),
                y_prev,
            )

    def ra_step3(r):
        ra_wait(r, 4)
        ra_wait(r, 5)
        ra_full(
            r, 8,
            [a_part(r, 0, True, h) + ra[r, 4, h].astype(F32) + ra[r, 5, h].astype(F32) for h in range(2)],
            y_pair,
        )

    def ra_final(r):
        for m in (6, 7, 8):
            ra_wait(r, m)
        for h in range(2):
            total = a_part(r, 0, False, h)
            for m in (6, 7, 8):
                total = total + ra[r, m, h].astype(F32)
            ga_out[:, r * RH + h * H : r * RH + (h + 1) * H] = total * a_scale

    def resp_copy(j, r):
        return pltpu.make_async_copy(
            resp_ref.at[r * RH : (r + 1) * RH, j * CJ : (j + 1) * CJ], rv.at[j, r], resp_sem.at[j * NR + r]
        )

    def front(t):
        j, r = TILES[t]
        resp_copy(j, r).wait()
        logits = jnp.dot(asc[r], dt[j], preferred_element_type=F32) + diff_ref[:, j * CJ : (j + 1) * CJ] * 0.5
        score = rv[j, r]
        sign = jnp.where(score == 2, -1.0, 1.0)
        rb[t % 2] = jnp.where(score > 0, jnp.tanh(logits) + sign, 0.0).astype(BF)

    seen_j, seen_r = set(), set()

    def back(t):
        j, r = TILES[t]
        residual = rb[t % 2]
        part_a = lax.dot_general(dt[j], residual, (((1,), (1,)), ((), ())), preferred_element_type=F32)
        part_d = jnp.dot(at[r], residual, preferred_element_type=F32)
        if r in seen_r:
            ga[r] += part_a
        else:
            ga[r] = part_a
        if j in seen_j:
            gd[j] += part_d
        else:
            gd[j] = part_d
        seen_r.add(r)
        seen_j.add(j)

    for j, r in TILES:
        resp_copy(j, r).start()
    for r in range(NR):
        at[r, pl.ds(a_rows(0, False, c), AB), :] = ability_ref[:, r * RH : (r + 1) * RH].astype(BF)
    for j in range(NJ):
        dt[j, pl.ds(d_rows(0, False), DB), :] = discrim_ref[:, j * CJ : (j + 1) * CJ].astype(BF)

    barrier = pltpu.get_barrier_semaphore()
    neighbours = (x_next, x_prev, x_pair, y_next, y_prev, y_pair, core)
    for device in neighbours:
        pl.semaphore_signal(barrier, inc=1, device_id=device, device_id_type=pl.DeviceIdType.MESH)
    pl.semaphore_wait(barrier, len(neighbours))

    a_step0(0)
    d_step0(0)
    d_step0(1)
    a_step0(1)
    d_step1(0)
    a_step1(0)
    d_step2(0)
    a_step2(0)
    d_step1(1)
    d_step0(2)
    a_step3(0)
    a_step1(1)
    d_step2(1)
    a_done(0)
    d_done(0)
    a_step2(1)
    front(0)
    d_done(1)
    front(1)
    back(0)
    a_step3(1)
    d_step1(2)
    d_step0(3)
    a_done(1)
    front(2)
    back(1)
    d_step2(2)
    d_step1(3)
    front(3)
    back(2)
    rd_step1(0)
    d_done(2)
    d_step2(3)
    front(4)
    back(3)
    rd_step1(1)
    rd_step2(0)
    d_done(3)
    front(5)
    back(4)
    rd_step3(0)
    rd_step2(1)
    front(6)
    back(5)
    ra_core(0)
    rd_step3(1)
    rd_final(0)
    front(7)
    back(6)
    rd_step1(2)
    ra_step1(0)
    rd_final(1)
    back(7)
    ra_core(1)
    rd_step1(3)
    rd_step2(2)
    ra_step2(0)
    ra_step1(1)
    rd_step2(3)
    rd_step3(2)
    ra_step3(0)
    ra_step2(1)
    rd_step3(3)
    ra_step3(1)
    rd_final(2)
    ra_final(0)
    rd_final(3)
    ra_final(1)
    for copy in sent:
        copy.wait_send()


def shards(response, difficulty, ability, ability_m, ability_v, discrim, discrim_m, discrim_v):
    vmem = pl.BlockSpec(memory_space=pltpu.VMEM)
    ga_t, gd_t = pl.pallas_call(
        kernel,
        out_shape=(jax.ShapeDtypeStruct((AB, N), F32), jax.ShapeDtypeStruct((DB, N), F32)),
        in_specs=[vmem, vmem, vmem, pl.BlockSpec(memory_space=pl.ANY)],
        out_specs=(vmem, vmem),
        scratch_shapes=[
            pltpu.VMEM((NR, K, RH), BF),
            pltpu.VMEM((NR, RH, K), BF),
            pltpu.VMEM((NJ, K, CJ), BF),
            pltpu.VMEM((NJ, NR, RH, CJ), jnp.int32),
            pltpu.VMEM((NR, K, RH), F32),
            pltpu.VMEM((NJ, K, CJ), F32),
            pltpu.VMEM((2, RH, CJ), BF),
            pltpu.VMEM((NJ, RD_MSG, DB, CJ), BF),
            pltpu.VMEM((NJ, RD_MSG, DB, CJ), BF),
            pltpu.VMEM((NR, RA_MSG, 2, AB, RH // 2), BF),
            pltpu.VMEM((NR, RA_MSG, 2, AB, RH // 2), BF),
            pltpu.VMEM((NR, 8, AB, RH), BF),
            pltpu.VMEM((NR, 8, AB, RH), BF),
            pltpu.SemaphoreType.DMA((N_SEM,)),
            pltpu.SemaphoreType.DMA((N_SEM,)),
            pltpu.SemaphoreType.DMA((NJ * NR,)),
        ],
        compiler_params=pltpu.CompilerParams(
            collective_id=0, has_side_effects=True, vmem_limit_bytes=60 << 20
        ),
        name="irt_step",
    )(ability.T, discrim.T, difficulty[None, :], response)
    ability_new, ability_m_new, ability_v_new = adam_update(ability, ability_m, ability_v, ga_t.T, 0.05)
    discrim_new, discrim_m_new, discrim_v_new = adam_update(discrim, discrim_m, discrim_v, gd_t.T, 0.01)
    return (ability_new, ability_m_new, ability_v_new, discrim_new, discrim_m_new, discrim_v_new)


def solution(mesh):
    return jax.shard_map(
        shards,
        mesh=mesh,
        in_specs=(
            P("mp", "item"),
            P("item"),
            P("mp", "item"),
            P("mp", "item"),
            P("mp", "item"),
            P("item", "mp"),
            P("item", "mp"),
            P("item", "mp"),
        ),
        out_specs=(
            P("mp", "item"),
            P("mp", "item"),
            P("mp", "item"),
            P("item", "mp"),
            P("item", "mp"),
            P("item", "mp"),
        ),
        check_vma=False,
    )
```

time: 387 us -> 65.2 us (0.17)
  waiting for transfers between devices: 324 us -> 0 us
  Pallas kernels: 0 us -> 60.6 us
  matrix products: 35.2 us -> 0 us
  between operations: 13.8 us -> 0.72 us
  local copies, waits for them, and re-layouts: 5.78 us -> 0.03 us
    psum x2 -> x0, waiting for transfers between devices: 236 us -> none  [the longest x1 130 us: shards(): ability_sum = lax.psum(ability_partial, 'item')]
    all_gather x2 -> x0, waiting for transfers between devices: 88.8 us -> none  [the longest x1 47.8 us: shards(): lax.all_gather(ability.astype(jnp.bfloat16), 'item', axis=1, tiled=True)]
    pallas_call x0 -> x1, Pallas kernels: none -> 60.6 us  [shards(): pl.pallas_call(kernel, out_shape=(jax.ShapeDtypeStruct((AB, N), F32), jax...]
    dot_general x3 -> x0, matrix products: 35.2 us -> none  [the longest x1 13.3 us: shards(): lax.dot_general(residual, ability_wide, (((0,), (0,)), ((), ())), precisi...]
    unnamed x18 -> x12, local copies, waits for them, and re-layouts: 5.78 us -> 0.03 us
  transfers between devices with their start and end apart: 4 -> 0, of which waited for: 4 -> 0; matrix products, arithmetic and copies ran while one was open for 4% -> 0% of each run, Pallas kernels for 0% -> 0%
where the time goes in v1:
time: 65.2 us; the launch traced here: 64.9 us
  Pallas kernels  60.6 us (93%)
  other arithmetic  3.62 us (6%)
  between operations  0.72 us (1%)
    pallas_call x1, Pallas kernels, shards(): pl.pallas_call(kernel, out_shape=(jax.ShapeDtypeStruct((AB, N), F32), jax...  60.6 us
    sub x2, other arithmetic, adam_update(): return (factor - step_rate * update, moment_new, second_new)  3.62 us

profile of v1, /device:TPU:0, one launch (start us, length us, event | category | flops | bytes accessed | tf_op | source)
XLA Modules:
  0.0 64.9 jit_solution(6718421751307151867)
XLA Ops:
  0.6 0.0 copy-start.1
  0.6 0.0 copy-start
  0.7 0.0 copy-start.2
  0.7 0.0 copy-start.3
  0.7 0.0 copy-start.4
  0.7 0.0 copy-start.5
  0.7 60.6 %irt_step.1 = (f32[16,2048]{1,0:T(8,128)}, f32[32,2048]{1,0:T(8,128)}) custom-call(f32[16,2048]{1,0:T(8,128)} %bitcast.18, f32[32,2048]{1,0:T(8,128)} %bitcast.17, f32[1,2048]{1,0:T(1,128)} %bitcast.19, s32[2048,2048]{1,0:T(8,128)} %resp_ref.1), custom_call_target="tpu_custom_call" | custom-call | tf_op jit(solution)/shard_map/irt_step/pallas_call | solution.py:430
  61.3 0.0 copy-done
  61.3 0.0 copy-done.2
  61.3 0.0 copy-done.3
  61.3 1.9 %multiply_subtract_fusion = (f32[2048,32]{0,1:T(8,128)}, f32[2048,32]{0,1:T(8,128)}, f32[2048,32]{0,1:T(8,128)}) fusion(f32[2048,32]{0,1:T(8,128)S(1)} %copy-done, f32[32,2048]{1,0:T(8,128)} %get-tuple-element.9, f32[2048,32]{0,1:T(8,128)S(1)} %copy-done.2, f32[2048,32]{0,1:T(8,128)S(1)} %copy-done.3), kind=kLoop, calls=%fused_computation.4 | loop fusion | flops 851968 | bytes 1835008 | tf_op jit(solution)/shard_map/sub | solution.py:42
  63.2 0.0 copy-done.1
  63.2 0.0 copy-done.4
  63.2 0.0 copy-done.5
  63.2 1.7 %multiply_subtract_fusion.1 = (f32[2048,16]{0,1:T(8,128)}, f32[2048,16]{0,1:T(8,128)}, f32[2048,16]{0,1:T(8,128)}) fusion(f32[2048,16]{0,1:T(8,128)S(1)} %copy-done.1, f32[16,2048]{1,0:T(8,128)} %get-tuple-element.8, f32[2048,16]{0,1:T(8,128)S(1)} %copy-done.4, f32[2048,16]{0,1:T(8,128)S(1)} %copy-done.5), kind=kLoop, calls=%fused_computation.9 | loop fusion | flops 425984 | bytes 917504 | tf_op jit(solution)/shard_map/sub | solution.py:42
Async XLA Ops:
  0.6 62.6 %copy-start.1 = (f32[2048,16]{0,1:T(8,128)S(1)}, f32[2048,16]{0,1:T(8,128)}, u32[]{:S(2)}) copy-start(f32[2048,16]{0,1:T(8,128)} %param.10) | copy-start | bytes 393220
  0.6 60.6 %copy-start = (f32[2048,32]{0,1:T(8,128)S(1)}, f32[2048,32]{0,1:T(8,128)}, u32[]{:S(2)}) copy-start(f32[2048,32]{0,1:T(8,128)} %param.13) | copy-start | bytes 786436
  0.7 60.6 %copy-start.2 = (f32[2048,32]{0,1:T(8,128)S(1)}, f32[2048,32]{0,1:T(8,128)}, u32[]{:S(2)}) copy-start(f32[2048,32]{0,1:T(8,128)} %param.14) | copy-start | bytes 786436
  0.7 60.6 %copy-start.3 = (f32[2048,32]{0,1:T(8,128)S(1)}, f32[2048,32]{0,1:T(8,128)}, u32[]{:S(2)}) copy-start(f32[2048,32]{0,1:T(8,128)} %param.15) | copy-start | bytes 786436
  0.7 62.6 %copy-start.4 = (f32[2048,16]{0,1:T(8,128)S(1)}, f32[2048,16]{0,1:T(8,128)}, u32[]{:S(2)}) copy-start(f32[2048,16]{0,1:T(8,128)} %param.11) | copy-start | bytes 393220
  0.7 62.5 %copy-start.5 = (f32[2048,16]{0,1:T(8,128)S(1)}, f32[2048,16]{0,1:T(8,128)}, u32[]{:S(2)}) copy-start(f32[2048,16]{0,1:T(8,128)} %param.12) | copy-start | bytes 393220

commit v2 on v0

v2 whole, which is shorter than its diff:
```python
import math

import jax
import jax.numpy as jnp
from jax import lax
from jax.experimental import pallas as pl
from jax.experimental.pallas import tpu as pltpu
from jax.sharding import PartitionSpec as P

K = 256
N = 2048
RH, CJ = 1024, 512
NR, NJ = N // RH, N // CJ
RING = 4
DB, AB = 32, 16
ROW = CJ * 4
BLOCK = DB * CJ * 2

TILES = ((0, 0), (1, 0), (0, 1), (1, 1), (2, 0), (3, 0), (2, 1), (3, 1))

G_D, G_A, S_D, S_A = 0, 3 * NJ, 3 * NJ + 3 * NR, 6 * NJ + 3 * NR
N_SEM = 6 * NJ + 6 * NR

beta_one = 0.9
beta_two = 0.999
corr_one = 1.0 - 0.9**10
corr_two = 1.0 - 0.999**10
adam_eps = 1e-08

BF = jnp.bfloat16
F32 = jnp.float32


def adam_update(factor, moment, second, gradient, step_rate):
    moment_new = beta_one * moment + (1.0 - beta_one) * gradient
    second_new = beta_two * second + (1.0 - beta_two) * gradient * gradient
    update = moment_new / corr_one / (jnp.sqrt(second_new / corr_two) + adam_eps)
    return (factor - step_rate * update, moment_new, second_new)


def kernel(
    ability_ref, discrim_ref, diff_ref, resp_ref, ga_out, gd_out,
    at, asc, dt, rv, ga, gd, rb, sd, rd, sa, ra, cs, cr,
    send_sem, recv_sem, resp_sem,
):
    mp, item = lax.axis_index("mp"), lax.axis_index("item")
    x, p = mp // 2, mp % 2
    z, y, c = item // 8, (item // 2) % RING, item % 2

    def mp_dev(dx, flip):
        return {"mp": ((x + dx) % RING) * 2 + (1 - p if flip else p)}

    def item_dev(dy, flip):
        return {"item": ((1 - z if flip else z) * RING + (y + dy) % RING) * 2 + c}

    xs = {d: mp_dev(d, False) for d in (1, 2, 3)}
    ys = {d: item_dev(d, False) for d in (1, 2, 3)}
    x_pair, y_pair = mp_dev(0, True), item_dev(0, True)
    core = {"item": item + 1 - 2 * c}

    sent_rows = [0, 0]

    def send(phase, index, src, dst, device):
        pltpu.make_async_remote_copy(
            src_ref=src, dst_ref=dst, send_sem=send_sem.at[phase], recv_sem=recv_sem.at[index],
            device_id=device, device_id_type=pl.DeviceIdType.MESH,
        ).start()
        sent_rows[phase] += math.prod(src.shape) * 2 // ROW

    def wait_rows(sem, rows):
        ref = rv.at[0, 0, pl.ds(0, rows)]
        pltpu.make_async_copy(ref, ref, sem).wait()

    def arrive(index, blocks):
        wait_rows(recv_sem.at[index], blocks * BLOCK // ROW)

    def d_rows(dx, flip):
        block = ((x + dx) % RING) * 2 + (1 - p if flip else p)
        return pl.multiple_of(block * DB, DB)

    def d_send(j, s, dx, flip, device):
        ref = dt.at[j, pl.ds(d_rows(dx, flip), DB), :]
        send(0, G_D + 3 * j + s, ref, ref, device)

    def d_step0(j):
        d_send(j, 0, 0, False, x_pair)
        d_send(j, 1, 0, False, xs[2])
        d_send(j, 2, 0, False, xs[1])
        d_send(j, 2, 0, False, xs[3])

    def d_step1(j):
        arrive(G_D + 3 * j, 1)
        d_send(j, 2, 0, True, xs[1])
        d_send(j, 2, 0, True, xs[3])

    def d_step2(j):
        arrive(G_D + 3 * j + 1, 1)
        d_send(j, 2, 2, False, x_pair)

    def d_done(j):
        arrive(G_D + 3 * j + 2, 5)

    def a_chip(dy, flip):
        return (1 - z if flip else z) * RING + (y + dy) % RING

    def a_send(r, s, dy, flip, device):
        ref = at.at[r, a_chip(dy, flip), c]
        send(0, G_A + 3 * r + s, ref, ref, device)

    def a_step0(r):
        a_send(r, 0, 0, False, y_pair)
        for d in (2, 1, 3):
            a_send(r, 1, 0, False, ys[d])

    def a_step1(r):
        arrive(G_A + 3 * r, 1)
        for d in (2, 1, 3):
            a_send(r, 1, 0, True, ys[d])

    def a_step2(r):
        arrive(G_A + 3 * r + 1, 6)
        ref = at.at[r, :, c]
        send(0, G_A + 3 * r + 2, ref, ref, core)

    def a_done(r):
        arrive(G_A + 3 * r + 2, 8)
        for i in range(RH // 512):
            part = at[r, :, :, :, i * 512 : (i + 1) * 512].reshape(K, 512).astype(F32) * 0.5
            asc[r, i * 512 : (i + 1) * 512, :] = part.T.astype(BF)

    def rd_send(j, m, s, value, device):
        sd[j, m] = value.astype(BF)
        send(1, S_D + 3 * j + s, sd.at[j, m], rd.at[j, m], device)

    def d_part(j, dx, flip):
        return gd[j, pl.ds(d_rows(dx, flip), DB), :]

    def d_in(j, m):
        return rd[j, m].astype(F32)

    def rd_step1(j):
        rd_send(j, 0, 0, d_part(j, 1, True), xs[1])
        rd_send(j, 1, 0, d_part(j, 3, True), xs[3])
        rd_send(j, 2, 1, d_part(j, 2, True), x_pair)
        rd_send(j, 3, 2, d_part(j, 1, False), xs[1])
        rd_send(j, 4, 2, d_part(j, 3, False), xs[3])

    def rd_step2(j):
        arrive(S_D + 3 * j + 1, 1)
        rd_send(j, 6, 2, d_part(j, 2, False) + d_in(j, 2), xs[2])
        arrive(S_D + 3 * j, 2)
        rd_send(j, 5, 2, d_part(j, 0, True) + d_in(j, 0) + d_in(j, 1), x_pair)

    d_scale = 0.5 * math.sqrt(1.0 / 16384)
    a_scale = 0.5 * math.sqrt(K / 32768)

    def rd_final(j):
        arrive(S_D + 3 * j + 2, 4)
        total = d_part(j, 0, False)
        for m in (3, 4, 5, 6):
            total = total + d_in(j, m)
        gd_out[:, j * CJ : (j + 1) * CJ] = total * d_scale

    def a_rows(chip, which):
        return pl.ds(pl.multiple_of((chip * 2 + which) * AB, AB), AB)

    def ra_core(r):
        for b in range(8):
            cs[r, b] = ga[r, a_rows(b, 1 - c), :].astype(BF)
        send(1, S_A + 3 * r, cs.at[r], cr.at[r], core)

    def a_part(r, dy, flip):
        chip = a_chip(dy, flip)
        return ga[r, a_rows(chip, c), :] + cr[r, chip].astype(F32)

    def ra_send(r, m, s, value, device):
        sa[r, m] = value.astype(BF)
        send(1, S_A + 3 * r + s, sa.at[r, m], ra.at[r, m], device)

    def ra_step1(r):
        arrive(S_A + 3 * r, 8)
        for d in (2, 1, 3):
            ra_send(r, d - 1, 1, a_part(r, d, True), ys[d])
        for d in (2, 1, 3):
            ra_send(r, d + 2, 2, a_part(r, d, False), ys[d])

    def ra_step2(r):
        arrive(S_A + 3 * r + 1, 3)
        total = a_part(r, 0, True)
        for m in (0, 1, 2):
            total = total + ra[r, m].astype(F32)
        ra_send(r, 6, 2, total, y_pair)

    def ra_final(r):
        arrive(S_A + 3 * r + 2, 4)
        total = a_part(r, 0, False)
        for m in (3, 4, 5, 6):
            total = total + ra[r, m].astype(F32)
        ga_out[:, r * RH : (r + 1) * RH] = total * a_scale

    def resp_copy(j, r):
        return pltpu.make_async_copy(
            resp_ref.at[r * RH : (r + 1) * RH, j * CJ : (j + 1) * CJ], rv.at[j, r], resp_sem.at[j * NR + r]
        )

    def front(t):
        j, r = TILES[t]
        resp_copy(j, r).wait()
        logits = jnp.dot(asc[r], dt[j], preferred_element_type=F32) + diff_ref[:, j * CJ : (j + 1) * CJ] * 0.5
        score = rv[j, r]
        sign = jnp.where(score == 2, -1.0, 1.0)
        rb[t % 2] = jnp.where(score > 0, jnp.tanh(logits) + sign, 0.0).astype(BF)

    seen_j, seen_r = set(), set()

    def back(t):
        j, r = TILES[t]
        residual = rb[t % 2]
        part_a = lax.dot_general(dt[j], residual, (((1,), (1,)), ((), ())), preferred_element_type=F32)
        part_d = jnp.dot(at[r].reshape(K, RH), residual, preferred_element_type=F32)
        if r in seen_r:
            ga[r] += part_a
        else:
            ga[r] = part_a
        if j in seen_j:
            gd[j] += part_d
        else:
            gd[j] = part_d
        seen_r.add(r)
        seen_j.add(j)

    for j, r in TILES:
        resp_copy(j, r).start()
    for r in range(NR):
        at[r, a_chip(0, False), c] = ability_ref[:, r * RH : (r + 1) * RH].astype(BF)
    for j in range(NJ):
        dt[j, pl.ds(d_rows(0, False), DB), :] = discrim_ref[:, j * CJ : (j + 1) * CJ].astype(BF)

    barrier = pltpu.get_barrier_semaphore()
    neighbours = (*xs.values(), x_pair, *ys.values(), y_pair, core)
    for device in neighbours:
        pl.semaphore_signal(barrier, inc=1, device_id=device, device_id_type=pl.DeviceIdType.MESH)
    pl.semaphore_wait(barrier, len(neighbours))

    a_step0(0)
    d_step0(0)
    d_step0(1)
    a_step0(1)
    d_step1(0)
    a_step1(0)
    d_step2(0)
    d_step0(2)
    d_step1(1)
    a_step1(1)
    d_step2(1)
    a_step2(0)
    d_step0(3)
    a_done(0)
    d_done(0)
    front(0)
    d_done(1)
    front(1)
    back(0)
    a_step2(1)
    d_step1(2)
    d_step2(2)
    a_done(1)
    front(2)
    back(1)
    d_step1(3)
    d_step2(3)
    front(3)
    back(2)
    rd_step1(0)
    d_done(2)
    front(4)
    back(3)
    rd_step1(1)
    rd_step2(0)
    d_done(3)
    front(5)
    back(4)
    rd_step2(1)
    front(6)
    back(5)
    ra_core(0)
    rd_final(0)
    front(7)
    back(6)
    rd_step1(2)
    ra_step1(0)
    rd_final(1)
    back(7)
    ra_core(1)
    rd_step1(3)
    rd_step2(2)
    ra_step1(1)
    ra_step2(0)
    rd_step2(3)
    ra_step2(1)
    rd_final(2)
    ra_final(0)
    rd_final(3)
    ra_final(1)
    for phase in range(2):
        wait_rows(send_sem.at[phase], sent_rows[phase])


def shards(response, difficulty, ability, ability_m, ability_v, discrim, discrim_m, discrim_v):
    vmem = pl.BlockSpec(memory_space=pltpu.VMEM)
    ga_t, gd_t = pl.pallas_call(
        kernel,
        out_shape=(jax.ShapeDtypeStruct((AB, N), F32), jax.ShapeDtypeStruct((DB, N), F32)),
        in_specs=[vmem, vmem, vmem, pl.BlockSpec(memory_space=pl.ANY)],
        out_specs=(vmem, vmem),
        scratch_shapes=[
            pltpu.VMEM((NR, 8, 2, AB, RH), BF),
            pltpu.VMEM((NR, RH, K), BF),
            pltpu.VMEM((NJ, K, CJ), BF),
            pltpu.VMEM((NJ, NR, RH, CJ), jnp.int32),
            pltpu.VMEM((NR, K, RH), F32),
            pltpu.VMEM((NJ, K, CJ), F32),
            pltpu.VMEM((2, RH, CJ), BF),
            pltpu.VMEM((NJ, 7, DB, CJ), BF),
            pltpu.VMEM((NJ, 7, DB, CJ), BF),
            pltpu.VMEM((NR, 7, AB, RH), BF),
            pltpu.VMEM((NR, 7, AB, RH), BF),
            pltpu.VMEM((NR, 8, AB, RH), BF),
            pltpu.VMEM((NR, 8, AB, RH), BF),
            pltpu.SemaphoreType.DMA((2,)),
            pltpu.SemaphoreType.DMA((N_SEM,)),
            pltpu.SemaphoreType.DMA((NJ * NR,)),
        ],
        compiler_params=pltpu.CompilerParams(
            collective_id=0, has_side_effects=True, vmem_limit_bytes=60 << 20
        ),
        name="irt_step",
    )(ability.T, discrim.T, difficulty[None, :], response)
    ability_new, ability_m_new, ability_v_new = adam_update(ability, ability_m, ability_v, ga_t.T, 0.05)
    discrim_new, discrim_m_new, discrim_v_new = adam_update(discrim, discrim_m, discrim_v, gd_t.T, 0.01)
    return (ability_new, ability_m_new, ability_v_new, discrim_new, discrim_m_new, discrim_v_new)


def solution(mesh):
    return jax.shard_map(
        shards,
        mesh=mesh,
        in_specs=(
            P("mp", "item"),
            P("item"),
            P("mp", "item"),
            P("mp", "item"),
            P("mp", "item"),
            P("item", "mp"),
            P("item", "mp"),
            P("item", "mp"),
        ),
        out_specs=(
            P("mp", "item"),
            P("mp", "item"),
            P("mp", "item"),
            P("item", "mp"),
            P("item", "mp"),
            P("item", "mp"),
        ),
        check_vma=False,
    )
```

time: 387 us -> 48.6 us (0.13)
  waiting for transfers between devices: 324 us -> 0 us
  Pallas kernels: 0 us -> 44.1 us
  matrix products: 35.2 us -> 0 us
  between operations: 13.8 us -> 0.72 us
  local copies, waits for them, and re-layouts: 5.78 us -> 0.03 us
    psum x2 -> x0, waiting for transfers between devices: 236 us -> none  [the longest x1 130 us: shards(): ability_sum = lax.psum(ability_partial, 'item')]
    all_gather x2 -> x0, waiting for transfers between devices: 88.8 us -> none  [the longest x1 47.8 us: shards(): lax.all_gather(ability.astype(jnp.bfloat16), 'item', axis=1, tiled=True)]
    pallas_call x0 -> x1, Pallas kernels: none -> 44.1 us  [shards(): pl.pallas_call(kernel, out_shape=(jax.ShapeDtypeStruct((AB, N), F32), jax...]
    dot_general x3 -> x0, matrix products: 35.2 us -> none  [the longest x1 13.3 us: shards(): lax.dot_general(residual, ability_wide, (((0,), (0,)), ((), ())), precisi...]
    unnamed x18 -> x12, local copies, waits for them, and re-layouts: 5.78 us -> 0.03 us
  transfers between devices with their start and end apart: 4 -> 0, of which waited for: 4 -> 0; matrix products, arithmetic and copies ran while one was open for 4% -> 0% of each run, Pallas kernels for 0% -> 0%
where the time goes in v2:
time: 48.6 us; the launch traced here: 48.5 us
  Pallas kernels  44.1 us (91%)
  other arithmetic  3.62 us (7%)
  between operations  0.72 us (1%)
    pallas_call x1, Pallas kernels, shards(): pl.pallas_call(kernel, out_shape=(jax.ShapeDtypeStruct((AB, N), F32), jax...  44.1 us
    sub x2, other arithmetic, adam_update(): return (factor - step_rate * update, moment_new, second_new)  3.62 us

profile of v2, /device:TPU:0, one launch (start us, length us, event | category | flops | bytes accessed | tf_op | source)
XLA Modules:
  0.0 48.5 jit_solution(2087024150372721086)
XLA Ops:
  0.6 0.0 copy-start.1
  0.6 0.0 copy-start
  0.7 0.0 copy-start.2
  0.7 0.0 copy-start.3
  0.7 0.0 copy-start.4
  0.7 0.0 copy-start.5
  0.7 44.1 %irt_step.1 = (f32[16,2048]{1,0:T(8,128)}, f32[32,2048]{1,0:T(8,128)}) custom-call(f32[16,2048]{1,0:T(8,128)} %bitcast.18, f32[32,2048]{1,0:T(8,128)} %bitcast.17, f32[1,2048]{1,0:T(1,128)} %bitcast.19, s32[2048,2048]{1,0:T(8,128)} %resp_ref.1), custom_call_target="tpu_custom_call" | custom-call | tf_op jit(solution)/shard_map/irt_step/pallas_call | solution.py:311
  44.8 0.0 copy-done
  44.8 0.0 copy-done.2
  44.8 0.0 copy-done.3
  44.8 1.9 %multiply_subtract_fusion = (f32[2048,32]{0,1:T(8,128)}, f32[2048,32]{0,1:T(8,128)}, f32[2048,32]{0,1:T(8,128)}) fusion(f32[2048,32]{0,1:T(8,128)S(1)} %copy-done, f32[32,2048]{1,0:T(8,128)} %get-tuple-element.9, f32[2048,32]{0,1:T(8,128)S(1)} %copy-done.2, f32[2048,32]{0,1:T(8,128)S(1)} %copy-done.3), kind=kLoop, calls=%fused_computation.4 | loop fusion | flops 851968 | bytes 1835008 | tf_op jit(solution)/shard_map/sub | solution.py:38
  46.8 0.0 copy-done.1
  46.8 0.0 copy-done.4
  46.8 0.0 copy-done.5
  46.8 1.7 %multiply_subtract_fusion.1 = (f32[2048,16]{0,1:T(8,128)}, f32[2048,16]{0,1:T(8,128)}, f32[2048,16]{0,1:T(8,128)}) fusion(f32[2048,16]{0,1:T(8,128)S(1)} %copy-done.1, f32[16,2048]{1,0:T(8,128)} %get-tuple-element.8, f32[2048,16]{0,1:T(8,128)S(1)} %copy-done.4, f32[2048,16]{0,1:T(8,128)S(1)} %copy-done.5), kind=kLoop, calls=%fused_computation.9 | loop fusion | flops 425984 | bytes 917504 | tf_op jit(solution)/shard_map/sub | solution.py:38
Async XLA Ops:
  0.6 46.1 %copy-start.1 = (f32[2048,16]{0,1:T(8,128)S(1)}, f32[2048,16]{0,1:T(8,128)}, u32[]{:S(2)}) copy-start(f32[2048,16]{0,1:T(8,128)} %param.10) | copy-start | bytes 393220
  0.6 44.2 %copy-start = (f32[2048,32]{0,1:T(8,128)S(1)}, f32[2048,32]{0,1:T(8,128)}, u32[]{:S(2)}) copy-start(f32[2048,32]{0,1:T(8,128)} %param.13) | copy-start | bytes 786436
  0.7 44.2 %copy-start.2 = (f32[2048,32]{0,1:T(8,128)S(1)}, f32[2048,32]{0,1:T(8,128)}, u32[]{:S(2)}) copy-start(f32[2048,32]{0,1:T(8,128)} %param.14) | copy-start | bytes 786436
  0.7 44.2 %copy-start.3 = (f32[2048,32]{0,1:T(8,128)S(1)}, f32[2048,32]{0,1:T(8,128)}, u32[]{:S(2)}) copy-start(f32[2048,32]{0,1:T(8,128)} %param.15) | copy-start | bytes 786436
  0.7 46.1 %copy-start.4 = (f32[2048,16]{0,1:T(8,128)S(1)}, f32[2048,16]{0,1:T(8,128)}, u32[]{:S(2)}) copy-start(f32[2048,16]{0,1:T(8,128)} %param.11) | copy-start | bytes 393220
  0.7 46.1 %copy-start.5 = (f32[2048,16]{0,1:T(8,128)S(1)}, f32[2048,16]{0,1:T(8,128)}, u32[]{:S(2)}) copy-start(f32[2048,16]{0,1:T(8,128)} %param.12) | copy-start | bytes 393220

commit v3 on v2

v3 whole, which is shorter than its diff:
```python
import math

import jax
import jax.numpy as jnp
from jax import lax
from jax.experimental import pallas as pl
from jax.experimental.pallas import tpu as pltpu
from jax.sharding import PartitionSpec as P

K = 256
N = 2048
ROWS = (512, 1024, 512)
COLS = (256, 768, 768, 256)
NR, NJ = len(ROWS), len(COLS)
ROW_AT = tuple(sum(ROWS[:r]) for r in range(NR))
COL_AT = tuple(sum(COLS[:j]) for j in range(NJ))
RING = 4
DB, AB = 32, 16
UNIT = 8 * 256 * 4

TILES = ((1, 0), (0, 0), (0, 1), (1, 1), (2, 1), (3, 1), (1, 2), (3, 0), (3, 2), (2, 0), (2, 2), (0, 2))

G_D, G_A, S_D, S_A = 0, 3 * NJ, 3 * NJ + 3 * NR, 6 * NJ + 3 * NR
N_SEM = 6 * NJ + 6 * NR
L_IN, L_OUT_A, L_OUT_D, L_RESP = 0, 3, 3 + NR, 3 + NR + NJ
N_LOCAL = 3 + NR + NJ + NR * NJ

beta_one = 0.9
beta_two = 0.999
corr_one = 1.0 - 0.9**10
corr_two = 1.0 - 0.999**10
adam_eps = 1e-08

BF = jnp.bfloat16
F32 = jnp.float32


def adam_update(factor, moment, second, gradient, step_rate):
    moment_new = beta_one * moment + (1.0 - beta_one) * gradient
    second_new = beta_two * second + (1.0 - beta_two) * gradient * gradient
    update = moment_new / corr_one / (jnp.sqrt(second_new / corr_two) + adam_eps)
    return (factor - step_rate * update, moment_new, second_new)


def kernel(ability_hbm, discrim_hbm, diff_hbm, resp_hbm, ga_hbm, gd_hbm, *scratch):
    scratch = list(scratch)

    def take(n):
        taken, scratch[:n] = scratch[:n], []
        return taken

    at, asc, ga, sa, ra, cs, cr = (take(NR) for _ in range(7))
    dt, gd, sd, rd = (take(NJ) for _ in range(4))
    rv, ability_ref, discrim_ref, diff_ref, ga_out, gd_out = take(6)
    rb = take(2)
    send_sem, recv_sem, local_sem = scratch

    mp, item = lax.axis_index("mp"), lax.axis_index("item")
    x, p = mp // 2, mp % 2
    z, y, c = item // 8, (item // 2) % RING, item % 2

    def mp_dev(dx, flip):
        return {"mp": ((x + dx) % RING) * 2 + (1 - p if flip else p)}

    def item_dev(dy, flip):
        return {"item": ((1 - z if flip else z) * RING + (y + dy) % RING) * 2 + c}

    xs = {d: mp_dev(d, False) for d in (1, 2, 3)}
    ys = {d: item_dev(d, False) for d in (1, 2, 3)}
    x_pair, y_pair = mp_dev(0, True), item_dev(0, True)
    core = {"item": item + 1 - 2 * c}

    sent_rows = [0, 0]

    def send(phase, index, src, dst, device):
        pltpu.make_async_remote_copy(
            src_ref=src, dst_ref=dst, send_sem=send_sem.at[phase], recv_sem=recv_sem.at[index],
            device_id=device, device_id_type=pl.DeviceIdType.MESH,
        ).start()
        sent_rows[phase] += math.prod(src.shape) * 2 // UNIT

    def wait_rows(sem, rows):
        ref = rv.at[0 : 8 * rows, 0:256]
        pltpu.make_async_copy(ref, ref, sem).wait()

    def arrive(index, blocks, block_bytes):
        wait_rows(recv_sem.at[index], blocks * block_bytes // UNIT)

    def d_rows(dx, flip):
        block = ((x + dx) % RING) * 2 + (1 - p if flip else p)
        return pl.multiple_of(block * DB, DB)

    def d_send(j, s, dx, flip, device):
        ref = dt[j].at[pl.ds(d_rows(dx, flip), DB), :]
        send(0, G_D + 3 * j + s, ref, ref, device)

    def d_step0(j):
        d_send(j, 0, 0, False, x_pair)
        d_send(j, 1, 0, False, xs[2])
        d_send(j, 2, 0, False, xs[1])
        d_send(j, 2, 0, False, xs[3])

    def d_step1(j):
        arrive(G_D + 3 * j, 1, DB * COLS[j] * 2)
        d_send(j, 2, 0, True, xs[1])
        d_send(j, 2, 0, True, xs[3])

    def d_step2(j):
        arrive(G_D + 3 * j + 1, 1, DB * COLS[j] * 2)
        d_send(j, 2, 2, False, x_pair)

    def d_done(j):
        arrive(G_D + 3 * j + 2, 5, DB * COLS[j] * 2)

    def a_chip(dy, flip):
        return (1 - z if flip else z) * RING + (y + dy) % RING

    def a_send(r, s, dy, flip, device):
        ref = at[r].at[a_chip(dy, flip), c]
        send(0, G_A + 3 * r + s, ref, ref, device)

    def a_step0(r):
        a_send(r, 0, 0, False, y_pair)
        for d in (2, 1, 3):
            a_send(r, 1, 0, False, ys[d])

    def a_step1(r):
        arrive(G_A + 3 * r, 1, AB * ROWS[r] * 2)
        for d in (2, 1, 3):
            a_send(r, 1, 0, True, ys[d])

    def a_step2(r):
        arrive(G_A + 3 * r + 1, 6, AB * ROWS[r] * 2)
        ref = at[r].at[:, c]
        send(0, G_A + 3 * r + 2, ref, ref, core)

    def a_done(r):
        arrive(G_A + 3 * r + 2, 8, AB * ROWS[r] * 2)
        for i in range(0, ROWS[r], 256):
            part = at[r][:, :, :, i : i + 256].reshape(K, 256).astype(F32) * 0.5
            asc[r][i : i + 256, :] = part.T.astype(BF)

    def rd_send(j, m, s, value, device):
        sd[j][m] = value.astype(BF)
        send(1, S_D + 3 * j + s, sd[j].at[m], rd[j].at[m], device)

    def d_part(j, dx, flip):
        return gd[j][pl.ds(d_rows(dx, flip), DB), :]

    def d_in(j, m):
        return rd[j][m].astype(F32)

    def rd_step1(j):
        rd_send(j, 0, 0, d_part(j, 1, True), xs[1])
        rd_send(j, 1, 0, d_part(j, 3, True), xs[3])
        rd_send(j, 2, 1, d_part(j, 2, True), x_pair)
        rd_send(j, 3, 2, d_part(j, 1, False), xs[1])
        rd_send(j, 4, 2, d_part(j, 3, False), xs[3])

    def rd_step2(j):
        arrive(S_D + 3 * j + 1, 1, DB * COLS[j] * 2)
        rd_send(j, 6, 2, d_part(j, 2, False) + d_in(j, 2), xs[2])
        arrive(S_D + 3 * j, 2, DB * COLS[j] * 2)
        rd_send(j, 5, 2, d_part(j, 0, True) + d_in(j, 0) + d_in(j, 1), x_pair)

    d_scale = 0.5 * math.sqrt(1.0 / 16384)
    a_scale = 0.5 * math.sqrt(K / 32768)

    def rd_final(j):
        arrive(S_D + 3 * j + 2, 4, DB * COLS[j] * 2)
        total = d_part(j, 0, False)
        for m in (3, 4, 5, 6):
            total = total + d_in(j, m)
        cols = slice(COL_AT[j], COL_AT[j] + COLS[j])
        gd_out[:, cols] = total * d_scale
        out_copy(gd_out, gd_hbm, cols, L_OUT_D + j).start()

    def a_rows(chip, which):
        return pl.ds(pl.multiple_of((chip * 2 + which) * AB, AB), AB)

    def ra_core(r):
        for b in range(8):
            cs[r][b] = ga[r][a_rows(b, 1 - c), :].astype(BF)
        send(1, S_A + 3 * r, cs[r], cr[r], core)

    def a_part(r, dy, flip):
        chip = a_chip(dy, flip)
        return ga[r][a_rows(chip, c), :] + cr[r][chip].astype(F32)

    def ra_send(r, m, s, value, device):
        sa[r][m] = value.astype(BF)
        send(1, S_A + 3 * r + s, sa[r].at[m], ra[r].at[m], device)

    def ra_step1(r):
        arrive(S_A + 3 * r, 8, AB * ROWS[r] * 2)
        for d in (2, 1, 3):
            ra_send(r, d - 1, 1, a_part(r, d, True), ys[d])
        for d in (2, 1, 3):
            ra_send(r, d + 2, 2, a_part(r, d, False), ys[d])

    def ra_step2(r):
        arrive(S_A + 3 * r + 1, 3, AB * ROWS[r] * 2)
        total = a_part(r, 0, True)
        for m in (0, 1, 2):
            total = total + ra[r][m].astype(F32)
        ra_send(r, 6, 2, total, y_pair)

    def ra_final(r):
        arrive(S_A + 3 * r + 2, 4, AB * ROWS[r] * 2)
        total = a_part(r, 0, False)
        for m in (3, 4, 5, 6):
            total = total + ra[r][m].astype(F32)
        cols = slice(ROW_AT[r], ROW_AT[r] + ROWS[r])
        ga_out[:, cols] = total * a_scale
        out_copy(ga_out, ga_hbm, cols, L_OUT_A + r).start()

    def resp_copy(j, r):
        rows, cols = slice(ROW_AT[r], ROW_AT[r] + ROWS[r]), slice(COL_AT[j], COL_AT[j] + COLS[j])
        return pltpu.make_async_copy(
            resp_hbm.at[rows, cols], rv.at[rows, cols], local_sem.at[L_RESP + j * NR + r]
        )

    def residual_of(t):
        j, r = TILES[t]
        return rb[t % 2].at[0 : ROWS[r], 0 : COLS[j]]

    def front(t):
        j, r = TILES[t]
        rows, cols = slice(ROW_AT[r], ROW_AT[r] + ROWS[r]), slice(COL_AT[j], COL_AT[j] + COLS[j])
        resp_copy(j, r).wait()
        logits = jnp.dot(asc[r][...], dt[j][...], preferred_element_type=F32) + diff_ref[:, cols] * 0.5
        score = rv[rows, cols]
        sign = jnp.where(score == 2, -1.0, 1.0)
        residual_of(t)[...] = jnp.where(score > 0, jnp.tanh(logits) + sign, 0.0).astype(BF)

    seen_j, seen_r = set(), set()

    def back(t):
        j, r = TILES[t]
        residual = residual_of(t)[...]
        part_a = lax.dot_general(dt[j][...], residual, (((1,), (1,)), ((), ())), preferred_element_type=F32)
        part_d = jnp.dot(at[r][...].reshape(K, ROWS[r]), residual, preferred_element_type=F32)
        if r in seen_r:
            ga[r][...] += part_a
        else:
            ga[r][...] = part_a
        if j in seen_j:
            gd[j][...] += part_d
        else:
            gd[j][...] = part_d
        seen_r.add(r)
        seen_j.add(j)

    def out_copy(src, dst, cols, index):
        return pltpu.make_async_copy(src.at[:, cols], dst.at[:, cols], local_sem.at[index])

    barrier = pltpu.get_barrier_semaphore()
    neighbours = (*xs.values(), x_pair, *ys.values(), y_pair, core)
    for device in neighbours:
        pl.semaphore_signal(barrier, inc=1, device_id=device, device_id_type=pl.DeviceIdType.MESH)

    inputs = [
        pltpu.make_async_copy(src, dst, local_sem.at[L_IN + i])
        for i, (src, dst) in enumerate(
            ((discrim_hbm, discrim_ref), (ability_hbm, ability_ref), (diff_hbm, diff_ref))
        )
    ]
    for copy in inputs:
        copy.start()
    for j, r in TILES:
        resp_copy(j, r).start()
    for copy in inputs:
        copy.wait()
    for r in range(NR):
        at[r][a_chip(0, False), c] = ability_ref[:, ROW_AT[r] : ROW_AT[r] + ROWS[r]].astype(BF)
    for j in range(NJ):
        dt[j][pl.ds(d_rows(0, False), DB), :] = discrim_ref[:, COL_AT[j] : COL_AT[j] + COLS[j]].astype(BF)
    pl.semaphore_wait(barrier, len(neighbours))

    a_step0(0)
    d_step0(0)
    a_step0(1)
    d_step0(1)
    a_step0(2)
    d_step0(2)
    d_step1(0)
    a_step1(0)
    d_step2(0)
    a_step1(1)
    d_step1(1)
    d_step2(1)
    a_step1(2)
    d_step0(3)
    d_step1(2)
    a_step2(0)
    d_step2(2)
    a_done(0)
    a_step2(1)
    d_step1(3)
    d_done(1)
    front(0)
    d_done(0)
    front(1)
    back(0)
    a_step2(2)
    a_done(1)
    d_step2(3)
    front(2)
    back(1)
    front(3)
    back(2)
    d_done(2)
    front(4)
    back(3)
    d_done(3)
    front(5)
    back(4)
    a_done(2)
    front(6)
    back(5)
    ra_core(1)
    front(7)
    back(6)
    rd_step1(1)
    front(8)
    back(7)
    front(9)
    back(8)
    ra_step1(1)
    rd_step1(3)
    front(10)
    back(9)
    ra_core(0)
    front(11)
    back(10)
    rd_step1(2)
    back(11)
    ra_core(2)
    rd_step1(0)
    rd_step2(1)
    ra_step1(0)
    ra_step1(2)
    ra_step2(1)
    rd_step2(3)
    rd_step2(2)
    ra_step2(0)
    rd_step2(0)
    ra_step2(2)
    ra_final(1)
    rd_final(1)
    rd_final(3)
    ra_final(0)
    rd_final(2)
    rd_final(0)
    ra_final(2)
    for phase in range(2):
        wait_rows(send_sem.at[phase], sent_rows[phase])
    for r in range(NR):
        out_copy(ga_out, ga_hbm, slice(ROW_AT[r], ROW_AT[r] + ROWS[r]), L_OUT_A + r).wait()
    for j in range(NJ):
        out_copy(gd_out, gd_hbm, slice(COL_AT[j], COL_AT[j] + COLS[j]), L_OUT_D + j).wait()


def adam_kernel(ga, a, am, av, gd, d, dm, dv, a_out, am_out, av_out, d_out, dm_out, dv_out):
    for grad, old, new, step_rate in (
        (ga, (a, am, av), (a_out, am_out, av_out), 0.05),
        (gd, (d, dm, dv), (d_out, dm_out, dv_out), 0.01),
    ):
        values = adam_update(old[0][...], old[1][...], old[2][...], grad[...], step_rate)
        for ref, value in zip(new, values):
            ref[...] = value


def shards(response, difficulty, ability, ability_m, ability_v, discrim, discrim_m, discrim_v):
    vmem = pl.BlockSpec(memory_space=pltpu.VMEM)
    hbm = pl.BlockSpec(memory_space=pl.ANY)
    grad_shapes = (jax.ShapeDtypeStruct((AB, N), F32), jax.ShapeDtypeStruct((DB, N), F32))
    ga_t, gd_t = pl.pallas_call(
        kernel,
        out_shape=grad_shapes,
        in_specs=[hbm] * 4,
        out_specs=(hbm, hbm),
        scratch_shapes=[
            *(pltpu.VMEM((8, 2, AB, h), BF) for h in ROWS),
            *(pltpu.VMEM((h, K), BF) for h in ROWS),
            *(pltpu.VMEM((K, h), F32) for h in ROWS),
            *(pltpu.VMEM((7, AB, h), BF) for h in ROWS),
            *(pltpu.VMEM((7, AB, h), BF) for h in ROWS),
            *(pltpu.VMEM((8, AB, h), BF) for h in ROWS),
            *(pltpu.VMEM((8, AB, h), BF) for h in ROWS),
            *(pltpu.VMEM((K, w), BF) for w in COLS),
            *(pltpu.VMEM((K, w), F32) for w in COLS),
            *(pltpu.VMEM((7, DB, w), BF) for w in COLS),
            *(pltpu.VMEM((7, DB, w), BF) for w in COLS),
            pltpu.VMEM((N, N), jnp.int32),
            pltpu.VMEM((AB, N), F32),
            pltpu.VMEM((DB, N), F32),
            pltpu.VMEM((1, N), F32),
            pltpu.VMEM((AB, N), F32),
            pltpu.VMEM((DB, N), F32),
            *(pltpu.VMEM((max(ROWS), max(COLS)), BF) for _ in range(2)),
            pltpu.SemaphoreType.DMA((2,)),
            pltpu.SemaphoreType.DMA((N_SEM,)),
            pltpu.SemaphoreType.DMA((N_LOCAL,)),
        ],
        compiler_params=pltpu.CompilerParams(
            collective_id=0, has_side_effects=True, vmem_limit_bytes=60 << 20
        ),
        name="irt_step",
    )(ability.T, discrim.T, difficulty[None, :], response)
    outs = pl.pallas_call(
        adam_kernel,
        out_shape=(grad_shapes[0],) * 3 + (grad_shapes[1],) * 3,
        in_specs=[vmem] * 8,
        out_specs=(vmem,) * 6,
        name="irt_adam",
    )(ga_t, ability.T, ability_m.T, ability_v.T, gd_t, discrim.T, discrim_m.T, discrim_v.T)
    return tuple(out.T for out in outs)


def solution(mesh):
    return jax.shard_map(
        shards,
        mesh=mesh,
        in_specs=(
            P("mp", "item"),
            P("item"),
            P("mp", "item"),
            P("mp", "item"),
            P("mp", "item"),
            P("item", "mp"),
            P("item", "mp"),
            P("item", "mp"),
        ),
        out_specs=(
            P("mp", "item"),
            P("mp", "item"),
            P("mp", "item"),
            P("item", "mp"),
            P("item", "mp"),
            P("item", "mp"),
        ),
        check_vma=False,
    )
```

time: 48.6 us -> 40.9 us (0.84)
  Pallas kernels: 44.1 us -> 40.1 us
  other arithmetic: 3.62 us -> 0 us
    pallas_call x1 -> x2, Pallas kernels: 44.1 us -> 40.1 us  [the longest x1 37.5 us: shards(): pl.pallas_call(kernel, out_shape=grad_shapes, in_specs=[hbm] * 4, out_spe...]
    sub x2 -> x0, other arithmetic: 3.62 us -> none  [adam_update(): return (factor - step_rate * update, moment_new, second_new)]
where the time goes in v3:
time: 40.9 us; the launch traced here: 40.7 us
  Pallas kernels  40.1 us (98%)
  between operations  0.64 us (2%)
    pallas_call x1, Pallas kernels, shards(): pl.pallas_call(kernel, out_shape=grad_shapes, in_specs=[hbm] * 4, out_spe...  37.5 us
    pallas_call x1, Pallas kernels, shards(): pl.pallas_call(adam_kernel, out_shape=(grad_shapes[0],) * 3 + (grad_shape...  2.57 us

profile of v3, /device:TPU:0, one launch (start us, length us, event | category | flops | bytes accessed | tf_op | source)
XLA Modules:
  0.0 40.7 jit_solution(9467233394798923594)
XLA Ops:
  0.6 37.5 %irt_step.1 = (f32[16,2048]{1,0:T(8,128)}, f32[32,2048]{1,0:T(8,128)}) custom-call(f32[16,2048]{1,0:T(8,128)} %bitcast.15, f32[32,2048]{1,0:T(8,128)} %bitcast.13, f32[1,2048]{1,0:T(1,128)} %bitcast.21, s32[2048,2048]{1,0:T(8,128)} %resp_hbm.1), custom_call_target="tpu_custom_call" | custom-call | tf_op jit(solution)/shard_map/irt_step/pallas_call | solution.py:378
  38.2 2.6 %irt_adam.1 = (f32[16,2048]{1,0:T(8,128)}, f32[16,2048]{1,0:T(8,128)}, f32[16,2048]{1,0:T(8,128)}, f32[32,2048]{1,0:T(8,128)}, f32[32,2048]{1,0:T(8,128)}, /*index=5*/f32[32,2048]{1,0:T(8,128)}) custom-call(f32[16,2048]{1,0:T(8,128)} %get-tuple-element.14.ga, f32[16,2048]{1,0:T(8,128)} %bitcast.16, f32[16,2048]{1,0:T(8,128)} %bitcast.19, ...), custom_call_target="tpu_custom_call" | custom-call | tf_op jit(solution)/shard_map/irt_adam/pallas_call | solution.py:411
